TPU v7x, 32 devices: a whole 2x2x4 slice. The times are simulated.
32 devices in a mesh: phase: 16 (over z, y, x), lat: 2 (over core).
Axes of the slice: x: 2, y: 2, z: 4, core: 2. Of those that a mesh axis runs over, the one named last changes fastest.
Arguments:
- state_now: float32 [3, 64, 1024], P(None, ('lat', 'phase')), may hold values from -4 to 4
- ocean_depth: float32 [64, 1024], P('lat'), may hold values from 0.5 to 1.5
- coriolis: float32 [64], P('lat'), may hold values from -0.4 to 0.4
- phase_times: float32 [16], P('phase'), may hold values from -6 to 6
- phase_weights: float32 [16], P('phase'), may hold values from 0.00625 to 0.25
Outputs:
- state_next: float32 [3, 64, 1024], P(None, ('lat', 'phase'))
- tendency: float32 [3, 64, 1024], P(None, ('lat', 'phase'))
All inputs are finite; a program needn't handle non-finite values.
Results may differ from a plain program's by a relative error of at most 0.00002.
Values sent between devices are 32-bit elements; how exact they have to be, the bound alone decides.
A program may use at most 64 MiB of HBM per device.

v0:
```python
import math
import jax
import jax.numpy as jnp
from jax import lax
from jax.sharding import PartitionSpec as P

DEG = 8
DEPTH = 4
radius_scale = 2.5
time_step = 0.5
series_terms = 20


def extended(shard, sides, width):
    for axis, dim in sides:
        devices, length = (lax.axis_size(axis), shard.shape[dim])
        up = [(i, (i + 1) % devices) for i in range(devices - 1)]
        down = [(j, i) for i, j in up]
        last = lax.slice_in_dim(shard, length - width, length, axis=dim)
        first = lax.slice_in_dim(shard, 0, width, axis=dim)
        before = lax.ppermute(last, axis, up)
        after = lax.ppermute(first, axis, down)
        shard = jnp.concatenate([before, shard, after], axis=dim)
    return shard


def along_lon(values):
    return (jnp.roll(values, -1, axis=-1) - jnp.roll(values, 1, axis=-1)) * 0.5


def along_lat(values):
    return (values[..., 2:, :] - values[..., :-2, :]) * 0.5


def interior(values):
    return values[..., 1:-1, :]


def wave_operator(fields, coefficients):
    height = fields[:, 0]
    eastward = fields[:, 1]
    northward = fields[:, 2]
    depth_field = coefficients[0]
    rotation = coefficients[1]
    out_height = -(along_lon(interior(depth_field * eastward)) + along_lat(depth_field * northward))
    out_east = -along_lon(interior(height)) + interior(rotation * northward)
    out_north = -along_lat(height) - interior(rotation * eastward)
    return jnp.stack([out_height, out_east, out_north], axis=1) / radius_scale


def advection(fields):
    height = fields[:, 0]
    eastward = fields[:, 1]
    northward = fields[:, 2]
    mid_east = interior(eastward)
    mid_north = interior(northward)
    out_height = -(along_lon(interior(height * eastward)) + along_lat(height * northward))
    out_east = -(mid_east * along_lon(mid_east) + mid_north * along_lat(eastward))
    out_north = -(mid_east * along_lon(mid_north) + mid_north * along_lat(northward))
    return jnp.stack([out_height, out_east, out_north], axis=1)


def series_coeffs(sample_time):
    half_time = sample_time * 0.5
    square = half_time * half_time
    result = []
    for degree in range(DEG + 1):
        summed = jnp.zeros_like(sample_time)
        term_sq = jnp.ones_like(sample_time)
        for series in range(series_terms):
            factor = (-1.0) ** series / (math.factorial(series) * math.factorial(series + degree))
            summed = summed + factor * term_sq
            term_sq = term_sq * square
        result.append(summed * half_time**degree)
    return result


def trimmed(values, have, wanted):
    excess = have - wanted
    if excess == 0:
        return values
    return values[:, :, excess : values.shape[2] - excess]


def per_device(state_now, ocean_depth, coriolis, phase_times, phase_weights):
    tile_rows = ocean_depth.shape[0]
    lat_count = lax.axis_size("lat")
    lat_place = lax.axis_index("lat")
    stacked = jnp.stack([ocean_depth, jnp.broadcast_to(coriolis[:, None], ocean_depth.shape)])
    coefficients = extended(stacked, (("lat", 1),), DEPTH)
    global_rows = lat_place * tile_rows - DEPTH + jnp.arange(tile_rows + 2 * DEPTH, dtype=jnp.int32)
    inside = ((global_rows >= 0) & (global_rows < tile_rows * lat_count)).astype(jnp.float32)
    forward = series_coeffs(phase_times)
    backward = series_coeffs(-phase_times)
    sample_count = phase_times.shape[0]

    def band_coeffs(margin):
        return coefficients[:, DEPTH - margin : DEPTH + tile_rows + margin]

    def band_inside(margin):
        return inside[DEPTH - margin : DEPTH + tile_rows + margin][None, None, :, None]

    def exponential(fields, series):
        accumulated = series[0][:, None, None, None] * fields
        previous = None
        current = fields
        width_prev = 0
        width_cur = 0
        for degree in range(1, DEG + 1):
            if (degree - 1) % DEPTH == 0:
                if previous is None:
                    current = extended(current, (("lat", 2),), DEPTH)
                else:
                    joined = jnp.concatenate(
                        [trimmed(previous, width_prev, 0), trimmed(current, width_cur, 0)], axis=0
                    )
                    joined = extended(joined, (("lat", 2),), DEPTH)
                    previous = joined[:sample_count]
                    current = joined[sample_count:]
                    width_prev = DEPTH
                width_cur = DEPTH
            width_new = width_cur - 1
            applied = wave_operator(current, band_coeffs(width_cur))
            if previous is None:
                advanced = applied
            else:
                advanced = 2.0 * applied + trimmed(previous, width_prev, width_new)
            advanced = advanced * band_inside(width_new)
            accumulated = accumulated + 2.0 * series[degree][:, None, None, None] * trimmed(
                advanced, width_new, 0
            )
            previous = current
            width_prev = width_cur
            current = advanced
            width_cur = width_new
        return accumulated

    def averaged(whole_tile):
        samples = whole_tile[None]
        waves = exponential(samples, forward)
        rimmed = extended(waves, (("lat", 2),), 1)
        pulled = advection(rimmed)
        returned = exponential(pulled, backward)
        return jnp.sum(phase_weights[:, None, None, None] * returned, axis=0)

    whole_tile = lax.all_gather(state_now, "phase", axis=1, tiled=True)

    def summed_whole(partial_value):
        return lax.psum(partial_value, "phase")

    first = summed_whole(averaged(whole_tile))
    middle = whole_tile + time_step * first
    second = summed_whole(averaged(middle))
    tendency_tile = 0.5 * (first + second)
    share = state_now.shape[1]
    start = lax.axis_index("phase") * share
    tendency = lax.dynamic_slice_in_dim(tendency_tile, start, share, 1)
    state_next = state_now + time_step * tendency
    return (state_next, tendency)


def solution(mesh):
    placed = (P(None, ("lat", "phase"), None), P("lat", None), P("lat"), P("phase"), P("phase"))
    return jax.shard_map(
        per_device,
        mesh=mesh,
        in_specs=placed,
        out_specs=(P(None, ("lat", "phase"), None), P(None, ("lat", "phase"), None)),
        check_vma=False,
    )
```

profile of v0, /device:TPU:0, one launch (start us, length us, event | category | flops | bytes accessed | tf_op | source)
XLA Modules:
  0.0 368.3 jit_solution(13352655160559666389)
XLA Ops:
  7.2 0.8 copy.168
  8.0 45.3 %all_gather.3 = f32[3,32,1024]{2,0,1:T(4,128)S(1)} all-gather(f32[3,2,1024]{2,0,1:T(4,128)S(1)} %copy.168), channel_id=1, replica_groups=mesh['phase'=16,'lat'=2] {'phase'}, dimensions={1}, use_global_device_ids=true | all-gather | bytes 417792 | tf_op jit(solution)/shard_map/all_gather | solution.py:146
  53.3 0.2 copy.179
  53.6 1.4 collective-permute-start.3
  55.0 3.0 collective-permute-start.2
  58.2 1.3 collective-permute-start.1
  59.5 3.0 collective-permute-start
  62.8 0.5 collective-permute-done
  64.0 0.2 fusion.311
  67.0 1.3 collective-permute-start.5
  68.3 3.0 collective-permute-start.4
  73.0 0.2 pad_maximum_fusion
  75.8 0.7 fusion.49
  76.5 1.3 collective-permute-start.7
  77.8 3.0 collective-permute-start.6
  80.9 0.8 collective-permute-done.6
  82.7 1.3 collective-permute-start.9
  84.0 3.0 collective-permute-start.8
  87.1 0.9 collective-permute-done.8
  91.5 1.3 collective-permute-start.11
  92.8 3.2 collective-permute-start.10
  97.5 0.2 pad_maximum_fusion.1
  100.2 1.3 fusion.41
  101.6 104.9 %all-reduce.3.cloned.1.call-done = f32[3,32,1024]{2,1,0:T(8,128)} async-done(((f32[3,32,1024]{2,1,0:T(8,128)}), f32[3,32,1024]{2,1,0:T(8,128)}) %all-reduce.3.cloned.1.call-update) | async-done | bytes 393232 | tf_op jit(solution)/shard_map/psum | solution.py:149
  206.5 1.2 fusion.500
  207.8 1.3 collective-permute-start.13
  209.1 3.0 collective-permute-start.12
  212.1 0.9 collective-permute-done.12
  216.6 1.3 collective-permute-start.15
  217.9 3.0 collective-permute-start.14
  220.9 0.9 collective-permute-done.14
  222.6 0.2 pad_maximum_fusion.2
  225.4 0.9 copy-done
  226.2 0.7 fusion.31
  227.0 1.3 collective-permute-start.17
  228.3 3.0 collective-permute-start.16
  231.3 0.8 collective-permute-done.16
  232.9 0.2 fusion.397
  233.2 1.3 collective-permute-start.19
  234.5 3.3 collective-permute-start.18
  237.8 0.6 collective-permute-done.18
  241.9 1.3 collective-permute-start.21
  243.2 3.0 collective-permute-start.20
  246.3 0.9 collective-permute-done.20
  247.9 0.2 pad_maximum_fusion.3
  250.7 1.3 fusion.23
  252.0 107.9 %all-reduce.5.cloned.1.call-done = f32[3,32,1024]{2,1,0:T(8,128)} async-done(((f32[3,32,1024]{2,1,0:T(8,128)}), f32[3,32,1024]{2,1,0:T(8,128)}) %all-reduce.5.cloned.1.call-update) | async-done | bytes 393232 | tf_op jit(solution)/shard_map/psum | solution.py:149
  359.9 1.5 multiply_add_fusion.1
  (356 shorter events, 28.4 us)
Async XLA Ops:
  7.2 199.3 %all-reduce.3.cloned.1.call-start = ((), (), s32[]{:S(2)}) async-start(), calls=%async_computation | async-start | bytes 786432 | tf_op jit(solution)/shard_map/psum | solution.py:149
  53.5 4.6 %copy-start.1 = (f32[32,1024]{1,0:T(8,128)S(1)}, f32[32,1024]{1,0:T(8,128)}, u32[]{:S(2)}) copy-start(f32[32,1024]{1,0:T(8,128)} %param.6) | copy-start | bytes 393220
  53.6 4.5 %copy-start.3 = (f32[32]{0:T(128)S(1)}, f32[32]{0:T(128)}, u32[]{:S(2)}) copy-start(f32[32]{0:T(128)} %param.7) | copy-start | bytes 388
  53.6 9.8 %collective-permute-start.3 = (f32[1,3,4,1024]{3,2,1,0:T(4,128)S(1)}, f32[1,3,4,1024]{3,2,1,0:T(4,128)S(1)}, u32[]{:S(2)}, u32[]{:S(2)}) collective-permute-start(f32[1,3,4,1024]{3,2,1,0:T(4,128)S(1)} %get-tuple-element.195), channel_id=1, source_target_pairs={{1,0},{3,2},{5,4},{7,6},{9,8},{11,10},{13,12},{15,14},{17,16},{19,... | collective-permute-start | bytes 147464 | tf_op jit(solution)/shard_map/ppermute | solution.py:22
  55.0 8.4 %collective-permute-start.2 = (f32[1,3,4,1024]{3,2,1,0:T(4,128)S(1)}, f32[1,3,4,1024]{3,2,1,0:T(4,128)S(1)}, u32[]{:S(2)}, u32[]{:S(2)}) collective-permute-start(f32[1,3,4,1024]{3,2,1,0:T(4,128)S(1)} %get-tuple-element.194), channel_id=1, source_target_pairs={{0,1},{2,3},{4,5},{6,7},{8,9},{10,11},{12,13},{14,15},{16,17},{18,... | collective-permute-start | bytes 147464 | tf_op jit(solution)/shard_map/ppermute | solution.py:21
  58.2 4.6 %collective-permute-start.1 = (f32[2,4,1024]{2,1,0:T(4,128)S(1)}, f32[2,4,1024]{2,1,0:T(4,128)S(1)}, u32[]{:S(2)}, u32[]{:S(2)}) collective-permute-start(f32[2,4,1024]{2,1,0:T(4,128)S(1)} %get-tuple-element.205), channel_id=1, source_target_pairs={{1,0},{3,2},{5,4},{7,6},{9,8},{11,10},{13,12},{15,14},{17,16},{19,... | collective-permute-start | bytes 98312 | tf_op jit(solution)/shard_map/ppermute | solution.py:22
  59.5 3.9 %collective-permute-start = (f32[2,4,1024]{2,1,0:T(4,128)S(1)}, f32[2,4,1024]{2,1,0:T(4,128)S(1)}, u32[]{:S(2)}, u32[]{:S(2)}) collective-permute-start(f32[2,4,1024]{2,1,0:T(4,128)S(1)} %get-tuple-element.204), channel_id=1, source_target_pairs={{0,1},{2,3},{4,5},{6,7},{8,9},{10,11},{12,13},{14,15},{16,17},{18,... | collective-permute-start | bytes 98312 | tf_op jit(solution)/shard_map/ppermute | solution.py:21
  67.0 5.3 %collective-permute-start.5 = (f32[2,3,4,1024]{3,2,1,0:T(4,128)S(1)}, f32[2,3,4,1024]{3,2,1,0:T(4,128)S(1)}, u32[]{:S(2)}, u32[]{:S(2)}) collective-permute-start(f32[2,3,4,1024]{3,2,1,0:T(4,128)S(1)} %get-tuple-element.91), channel_id=1, source_target_pairs={{1,0},{3,2},{5,4},{7,6},{9,8},{11,10},{13,12},{15,14},{17,16},{19,... | collective-permute-start | bytes 294920 | tf_op jit(solution)/shard_map/ppermute | solution.py:22
  68.3 4.0 %collective-permute-start.4 = (f32[2,3,4,1024]{3,2,1,0:T(4,128)S(1)}, f32[2,3,4,1024]{3,2,1,0:T(4,128)S(1)}, u32[]{:S(2)}, u32[]{:S(2)}) collective-permute-start(f32[2,3,4,1024]{3,2,1,0:T(4,128)S(1)} %get-tuple-element.90), channel_id=1, source_target_pairs={{0,1},{2,3},{4,5},{6,7},{8,9},{10,11},{12,13},{14,15},{16,17},{18,... | collective-permute-start | bytes 294920 | tf_op jit(solution)/shard_map/ppermute | solution.py:21
  76.5 4.3 %collective-permute-start.7 = (f32[1,3,1,1024]{3,2,1,0:T(1,128)S(1)}, f32[1,3,1,1024]{3,2,1,0:T(1,128)S(1)}, u32[]{:S(2)}, u32[]{:S(2)}) collective-permute-start(f32[1,3,1,1024]{3,2,1,0:T(1,128)S(1)} %get-tuple-element.193), channel_id=1, source_target_pairs={{1,0},{3,2},{5,4},{7,6},{9,8},{11,10},{13,12},{15,14},{17,16},{19,... | collective-permute-start | bytes 36872 | tf_op jit(solution)/shard_map/ppermute | solution.py:22
  77.8 3.9 %collective-permute-start.6 = (f32[1,3,1,1024]{3,2,1,0:T(1,128)S(1)}, f32[1,3,1,1024]{3,2,1,0:T(1,128)S(1)}, u32[]{:S(2)}, u32[]{:S(2)}) collective-permute-start(f32[1,3,1,1024]{3,2,1,0:T(1,128)S(1)} %get-tuple-element.192), channel_id=1, source_target_pairs={{0,1},{2,3},{4,5},{6,7},{8,9},{10,11},{12,13},{14,15},{16,17},{18,... | collective-permute-start | bytes 36872 | tf_op jit(solution)/shard_map/ppermute | solution.py:21
  82.7 4.3 %collective-permute-start.9 = (f32[1,3,4,1024]{3,2,1,0:T(4,128)S(1)}, f32[1,3,4,1024]{3,2,1,0:T(4,128)S(1)}, u32[]{:S(2)}, u32[]{:S(2)}) collective-permute-start(f32[1,3,4,1024]{3,2,1,0:T(4,128)S(1)} %get-tuple-element.191), channel_id=1, source_target_pairs={{1,0},{3,2},{5,4},{7,6},{9,8},{11,10},{13,12},{15,14},{17,16},{19,... | collective-permute-start | bytes 147464 | tf_op jit(solution)/shard_map/ppermute | solution.py:22
  84.0 3.9 %collective-permute-start.8 = (f32[1,3,4,1024]{3,2,1,0:T(4,128)S(1)}, f32[1,3,4,1024]{3,2,1,0:T(4,128)S(1)}, u32[]{:S(2)}, u32[]{:S(2)}) collective-permute-start(f32[1,3,4,1024]{3,2,1,0:T(4,128)S(1)} %get-tuple-element.190), channel_id=1, source_target_pairs={{0,1},{2,3},{4,5},{6,7},{8,9},{10,11},{12,13},{14,15},{16,17},{18,... | collective-permute-start | bytes 147464 | tf_op jit(solution)/shard_map/ppermute | solution.py:21
  91.5 5.2 %collective-permute-start.11 = (f32[2,3,4,1024]{3,2,1,0:T(4,128)S(1)}, f32[2,3,4,1024]{3,2,1,0:T(4,128)S(1)}, u32[]{:S(2)}, u32[]{:S(2)}) collective-permute-start(f32[2,3,4,1024]{3,2,1,0:T(4,128)S(1)} %get-tuple-element.89), channel_id=1, source_target_pairs={{1,0},{3,2},{5,4},{7,6},{9,8},{11,10},{13,12},{15,14},{17,16},{19,... | collective-permute-start | bytes 294920 | tf_op jit(solution)/shard_map/ppermute | solution.py:22
  92.8 4.0 %collective-permute-start.10 = (f32[2,3,4,1024]{3,2,1,0:T(4,128)S(1)}, f32[2,3,4,1024]{3,2,1,0:T(4,128)S(1)}, u32[]{:S(2)}, u32[]{:S(2)}) collective-permute-start(f32[2,3,4,1024]{3,2,1,0:T(4,128)S(1)} %get-tuple-element.88), channel_id=1, source_target_pairs={{0,1},{2,3},{4,5},{6,7},{8,9},{10,11},{12,13},{14,15},{16,17},{18,... | collective-permute-start | bytes 294920 | tf_op jit(solution)/shard_map/ppermute | solution.py:21
  101.6 258.3 %all-reduce.5.cloned.1.call-start = ((), (), s32[]{:S(2)}) async-start(), calls=%async_computation.1 | async-start | bytes 786432 | tf_op jit(solution)/shard_map/psum | solution.py:149
  207.8 4.3 %collective-permute-start.13 = (f32[1,3,4,1024]{3,2,1,0:T(4,128)S(1)}, f32[1,3,4,1024]{3,2,1,0:T(4,128)S(1)}, u32[]{:S(2)}, u32[]{:S(2)}) collective-permute-start(f32[1,3,4,1024]{3,2,1,0:T(4,128)S(1)} %get-tuple-element.189), channel_id=1, source_target_pairs={{1,0},{3,2},{5,4},{7,6},{9,8},{11,10},{13,12},{15,14},{17,16},{19,... | collective-permute-start | bytes 147464 | tf_op jit(solution)/shard_map/ppermute | solution.py:22
  209.1 3.9 %collective-permute-start.12 = (f32[1,3,4,1024]{3,2,1,0:T(4,128)S(1)}, f32[1,3,4,1024]{3,2,1,0:T(4,128)S(1)}, u32[]{:S(2)}, u32[]{:S(2)}) collective-permute-start(f32[1,3,4,1024]{3,2,1,0:T(4,128)S(1)} %get-tuple-element.188), channel_id=1, source_target_pairs={{0,1},{2,3},{4,5},{6,7},{8,9},{10,11},{12,13},{14,15},{16,17},{18,... | collective-permute-start | bytes 147464 | tf_op jit(solution)/shard_map/ppermute | solution.py:21
  216.6 4.3 %collective-permute-start.15 = (f32[2,3,4,1024]{3,2,1,0:T(4,128)S(1)}, f32[2,3,4,1024]{3,2,1,0:T(4,128)S(1)}, u32[]{:S(2)}, u32[]{:S(2)}) collective-permute-start(f32[2,3,4,1024]{3,2,1,0:T(4,128)S(1)} %get-tuple-element.87), channel_id=1, source_target_pairs={{1,0},{3,2},{5,4},{7,6},{9,8},{11,10},{13,12},{15,14},{17,16},{19,... | collective-permute-start | bytes 294920 | tf_op jit(solution)/shard_map/ppermute | solution.py:22
  217.9 4.0 %collective-permute-start.14 = (f32[2,3,4,1024]{3,2,1,0:T(4,128)S(1)}, f32[2,3,4,1024]{3,2,1,0:T(4,128)S(1)}, u32[]{:S(2)}, u32[]{:S(2)}) collective-permute-start(f32[2,3,4,1024]{3,2,1,0:T(4,128)S(1)} %get-tuple-element.86), channel_id=1, source_target_pairs={{0,1},{2,3},{4,5},{6,7},{8,9},{10,11},{12,13},{14,15},{16,17},{18,... | collective-permute-start | bytes 294920 | tf_op jit(solution)/shard_map/ppermute | solution.py:21
  225.2 1.0 copy-start
  227.0 4.3 %collective-permute-start.17 = (f32[1,3,1,1024]{3,2,1,0:T(1,128)S(1)}, f32[1,3,1,1024]{3,2,1,0:T(1,128)S(1)}, u32[]{:S(2)}, u32[]{:S(2)}) collective-permute-start(f32[1,3,1,1024]{3,2,1,0:T(1,128)S(1)} %get-tuple-element.187), channel_id=1, source_target_pairs={{1,0},{3,2},{5,4},{7,6},{9,8},{11,10},{13,12},{15,14},{17,16},{19,... | collective-permute-start | bytes 36872 | tf_op jit(solution)/shard_map/ppermute | solution.py:22
  228.3 3.9 %collective-permute-start.16 = (f32[1,3,1,1024]{3,2,1,0:T(1,128)S(1)}, f32[1,3,1,1024]{3,2,1,0:T(1,128)S(1)}, u32[]{:S(2)}, u32[]{:S(2)}) collective-permute-start(f32[1,3,1,1024]{3,2,1,0:T(1,128)S(1)} %get-tuple-element.186), channel_id=1, source_target_pairs={{0,1},{2,3},{4,5},{6,7},{8,9},{10,11},{12,13},{14,15},{16,17},{18,... | collective-permute-start | bytes 36872 | tf_op jit(solution)/shard_map/ppermute | solution.py:21
  233.2 4.6 %collective-permute-start.19 = (f32[1,3,4,1024]{3,2,1,0:T(4,128)S(1)}, f32[1,3,4,1024]{3,2,1,0:T(4,128)S(1)}, u32[]{:S(2)}, u32[]{:S(2)}) collective-permute-start(f32[1,3,4,1024]{3,2,1,0:T(4,128)S(1)} %get-tuple-element.185), channel_id=1, source_target_pairs={{1,0},{3,2},{5,4},{7,6},{9,8},{11,10},{13,12},{15,14},{17,16},{19,... | collective-permute-start | bytes 147464 | tf_op jit(solution)/shard_map/ppermute | solution.py:22
  234.5 3.9 %collective-permute-start.18 = (f32[1,3,4,1024]{3,2,1,0:T(4,128)S(1)}, f32[1,3,4,1024]{3,2,1,0:T(4,128)S(1)}, u32[]{:S(2)}, u32[]{:S(2)}) collective-permute-start(f32[1,3,4,1024]{3,2,1,0:T(4,128)S(1)} %get-tuple-element.184), channel_id=1, source_target_pairs={{0,1},{2,3},{4,5},{6,7},{8,9},{10,11},{12,13},{14,15},{16,17},{18,... | collective-permute-start | bytes 147464 | tf_op jit(solution)/shard_map/ppermute | solution.py:21
  241.9 4.3 %collective-permute-start.21 = (f32[2,3,4,1024]{3,2,1,0:T(4,128)S(1)}, f32[2,3,4,1024]{3,2,1,0:T(4,128)S(1)}, u32[]{:S(2)}, u32[]{:S(2)}) collective-permute-start(f32[2,3,4,1024]{3,2,1,0:T(4,128)S(1)} %get-tuple-element.85), channel_id=1, source_target_pairs={{1,0},{3,2},{5,4},{7,6},{9,8},{11,10},{13,12},{15,14},{17,16},{19,... | collective-permute-start | bytes 294920 | tf_op jit(solution)/shard_map/ppermute | solution.py:22
  243.2 4.0 %collective-permute-start.20 = (f32[2,3,4,1024]{3,2,1,0:T(4,128)S(1)}, f32[2,3,4,1024]{3,2,1,0:T(4,128)S(1)}, u32[]{:S(2)}, u32[]{:S(2)}) collective-permute-start(f32[2,3,4,1024]{3,2,1,0:T(4,128)S(1)} %get-tuple-element.84), channel_id=1, source_target_pairs={{0,1},{2,3},{4,5},{6,7},{8,9},{10,11},{12,13},{14,15},{16,17},{18,... | collective-permute-start | bytes 294920 | tf_op jit(solution)/shard_map/ppermute | solution.py:21
  252.0 107.9 %copy-start.2 = (f32[3,2,1024]{2,1,0:T(2,128)S(1)}, f32[3,2,1024]{2,1,0:T(2,128)}, u32[]{:S(2)}) copy-start(f32[3,2,1024]{2,1,0:T(2,128)} %param.5) | copy-start | bytes 73732
Sparse Core Ops, SparseCore 0:
  101.7 104.7 all-reduce.2
  252.1 107.7 all-reduce.4
where the time goes:
time: 369 us; the launch traced here: 368 us
  waiting for transfers between devices  219 us (59%)
  starting transfers between devices  48.2 us (13%)
  blocking collectives  45.3 us (12%)
  other arithmetic  21.8 us (6%)
  between operations  17.7 us (5%)
  local copies, waits for them, and re-layouts  16.1 us (4%)
    psum x2, waiting for transfers between devices, summed_whole(): return lax.psum(partial_value, 'phase')  213 us
    all_gather x1, blocking collectives, per_device(): whole_tile = lax.all_gather(state_now, 'phase', axis=1, tiled=True)  45.3 us
    ppermute x11, starting transfers between devices, extended(): before = lax.ppermute(last, axis, up)  33.8 us
    ppermute x11, starting transfers between devices, extended(): after = lax.ppermute(first, axis, down)  14.3 us
    slice x140, local copies, waits for them, and re-layouts, along_lon(): return (jnp.roll(values, -1, axis=-1) - jnp.roll(values, 1, axis=-1)) * 0.5  12.7 us
    another operation x63, other arithmetic, wave_operator(): return jnp.stack([out_height, out_east, out_north], axis=1) / radius_scale  7.91 us
  transfers between devices with their start and end apart: 24, of which 10 were waited for; matrix products, arithmetic and copies ran while one was open for 0% of the time, Pallas kernels for 0%

commit v1 on v0

--- a/solution.py
+++ b/solution.py
@@ -143,7 +143,14 @@
         returned = exponential(pulled, backward)
         return jnp.sum(phase_weights[:, None, None, None] * returned, axis=0)
 
-    whole_tile = lax.all_gather(state_now, "phase", axis=1, tiled=True)
+    ring = [state_now]
+    for hop in range(15):
+        ring.append(lax.ppermute(ring[-1], "phase", [(dev, (dev + 1) % 16) for dev in range(16)]))
+    whole_tile = jnp.roll(
+        jnp.concatenate(ring[::-1], axis=1),
+        (lax.axis_index("phase") + 1) * ring[0].shape[1],
+        axis=1,
+    )
 
     def summed_whole(partial_value):
         return lax.psum(partial_value, "phase")

time: 369 us -> 431 us (1.17)
  waiting for transfers between devices: 219 us -> 324 us
  blocking collectives: 45.3 us -> 0 us
    ppermute x0 -> x15, waiting for transfers between devices: none -> 105 us  [per_device(): lax.ppermute(ring[-1], 'phase', [(dev, (dev + 1) % 16) for dev in range(1...]
    all_gather x1 -> x0, blocking collectives: 45.3 us -> none  [per_device(): whole_tile = lax.all_gather(state_now, 'phase', axis=1, tiled=True)]
  transfers between devices with their start and end apart: 24 -> 39, of which waited for: 10 -> 26; matrix products, arithmetic and copies ran while one was open for 0% -> 0% of each run, Pallas kernels for 0% -> 0%
where the time goes in v1:
time: 431 us
  waiting for transfers between devices  324 us (75%)
  starting transfers between devices  51.1 us (12%)
  other arithmetic  21.2 us (5%)
  between operations  17.7 us (4%)
  local copies, waits for them, and re-layouts  16.5 us (4%)
    psum x2, waiting for transfers between devices, summed_whole(): return lax.psum(partial_value, 'phase')  213 us
    ppermute x15, waiting for transfers between devices, per_device(): lax.ppermute(ring[-1], 'phase', [(dev, (dev + 1) % 16) for dev in range(1...  105 us
    ppermute x11, starting transfers between devices, extended(): before = lax.ppermute(last, axis, up)  33.8 us
    ppermute x11, starting transfers between devices, extended(): after = lax.ppermute(first, axis, down)  14.2 us
    slice x140, local copies, waits for them, and re-layouts, along_lon(): return (jnp.roll(values, -1, axis=-1) - jnp.roll(values, 1, axis=-1)) * 0.5  12.7 us
  transfers between devices with their start and end apart: 39, of which 26 were waited for; matrix products, arithmetic and copies ran while one was open for 0% of the time, Pallas kernels for 0%

profile of v1, /device:TPU:0, one launch (start us, length us, event | category | flops | bytes accessed | tf_op | source)
XLA Modules:
  0.0 430.5 jit_solution(4660687579214937369)
XLA Ops:
  7.2 3.0 collective-permute-start
  10.2 6.0 %collective-permute-done = f32[3,2,1024]{2,1,0:T(2,128)S(1)} collective-permute-done((f32[3,2,1024]{2,1,0:T(2,128)}, f32[3,2,1024]{2,1,0:T(2,128)S(1)}, u32[]{:S(2)}, u32[]{:S(2)}) %collective-permute-start) | collective-permute-done | bytes 24608 | tf_op jit(solution)/shard_map/ppermute | solution.py:148
  16.3 7.4 %collective-permute-done.1 = f32[3,2,1024]{2,1,0:T(2,128)S(1)} collective-permute-done((f32[3,2,1024]{2,1,0:T(2,128)S(1)}, f32[3,2,1024]{2,1,0:T(2,128)S(1)}, u32[]{:S(2)}, u32[]{:S(2)}) %collective-permute-start.1) | collective-permute-done | bytes 24608 | tf_op jit(solution)/shard_map/ppermute | solution.py:148
  23.7 7.4 %collective-permute-done.2 = f32[3,2,1024]{2,1,0:T(2,128)S(1)} collective-permute-done((f32[3,2,1024]{2,1,0:T(2,128)S(1)}, f32[3,2,1024]{2,1,0:T(2,128)S(1)}, u32[]{:S(2)}, u32[]{:S(2)}) %collective-permute-start.2) | collective-permute-done | bytes 24608 | tf_op jit(solution)/shard_map/ppermute | solution.py:148
  31.1 7.4 %collective-permute-done.3 = f32[3,2,1024]{2,1,0:T(2,128)S(1)} collective-permute-done((f32[3,2,1024]{2,1,0:T(2,128)S(1)}, f32[3,2,1024]{2,1,0:T(2,128)S(1)}, u32[]{:S(2)}, u32[]{:S(2)}) %collective-permute-start.3) | collective-permute-done | bytes 24608 | tf_op jit(solution)/shard_map/ppermute | solution.py:148
  38.5 7.4 %collective-permute-done.4 = f32[3,2,1024]{2,1,0:T(2,128)S(1)} collective-permute-done((f32[3,2,1024]{2,1,0:T(2,128)S(1)}, f32[3,2,1024]{2,1,0:T(2,128)S(1)}, u32[]{:S(2)}, u32[]{:S(2)}) %collective-permute-start.4) | collective-permute-done | bytes 24608 | tf_op jit(solution)/shard_map/ppermute | solution.py:148
  45.9 7.4 %collective-permute-done.5 = f32[3,2,1024]{2,1,0:T(2,128)S(1)} collective-permute-done((f32[3,2,1024]{2,1,0:T(2,128)S(1)}, f32[3,2,1024]{2,1,0:T(2,128)S(1)}, u32[]{:S(2)}, u32[]{:S(2)}) %collective-permute-start.5) | collective-permute-done | bytes 24608 | tf_op jit(solution)/shard_map/ppermute | solution.py:148
  53.4 7.4 %collective-permute-done.6 = f32[3,2,1024]{2,1,0:T(2,128)S(1)} collective-permute-done((f32[3,2,1024]{2,1,0:T(2,128)S(1)}, f32[3,2,1024]{2,1,0:T(2,128)S(1)}, u32[]{:S(2)}, u32[]{:S(2)}) %collective-permute-start.6) | collective-permute-done | bytes 24608 | tf_op jit(solution)/shard_map/ppermute | solution.py:148
  60.8 7.4 %collective-permute-done.7 = f32[3,2,1024]{2,1,0:T(2,128)S(1)} collective-permute-done((f32[3,2,1024]{2,1,0:T(2,128)S(1)}, f32[3,2,1024]{2,1,0:T(2,128)S(1)}, u32[]{:S(2)}, u32[]{:S(2)}) %collective-permute-start.7) | collective-permute-done | bytes 24608 | tf_op jit(solution)/shard_map/ppermute | solution.py:148
  68.2 7.4 %collective-permute-done.8 = f32[3,2,1024]{2,1,0:T(2,128)S(1)} collective-permute-done((f32[3,2,1024]{2,1,0:T(2,128)S(1)}, f32[3,2,1024]{2,1,0:T(2,128)S(1)}, u32[]{:S(2)}, u32[]{:S(2)}) %collective-permute-start.8) | collective-permute-done | bytes 24608 | tf_op jit(solution)/shard_map/ppermute | solution.py:148
  75.6 7.4 %collective-permute-done.9 = f32[3,2,1024]{2,1,0:T(2,128)S(1)} collective-permute-done((f32[3,2,1024]{2,1,0:T(2,128)S(1)}, f32[3,2,1024]{2,1,0:T(2,128)S(1)}, u32[]{:S(2)}, u32[]{:S(2)}) %collective-permute-start.9) | collective-permute-done | bytes 24608 | tf_op jit(solution)/shard_map/ppermute | solution.py:148
  83.1 7.5 %collective-permute-done.10 = f32[3,2,1024]{2,1,0:T(2,128)S(1)} collective-permute-done((f32[3,2,1024]{2,1,0:T(2,128)S(1)}, f32[3,2,1024]{2,1,0:T(2,128)S(1)}, u32[]{:S(2)}, u32[]{:S(2)}) %collective-permute-start.10) | collective-permute-done | bytes 24608 | tf_op jit(solution)/shard_map/ppermute | solution.py:148
  90.6 7.4 %collective-permute-done.11 = f32[3,2,1024]{2,1,0:T(2,128)S(1)} collective-permute-done((f32[3,2,1024]{2,1,0:T(2,128)S(1)}, f32[3,2,1024]{2,1,0:T(2,128)S(1)}, u32[]{:S(2)}, u32[]{:S(2)}) %collective-permute-start.11) | collective-permute-done | bytes 24608 | tf_op jit(solution)/shard_map/ppermute | solution.py:148
  98.7 1.3 collective-permute-start.16
  100.0 3.0 collective-permute-start.15
  103.1 2.3 collective-permute-done.12
  105.4 7.4 %collective-permute-done.13 = f32[3,2,1024]{2,1,0:T(2,128)S(1)} collective-permute-done((f32[3,2,1024]{2,1,0:T(2,128)S(1)}, f32[3,2,1024]{2,1,0:T(2,128)S(1)}, u32[]{:S(2)}, u32[]{:S(2)}) %collective-permute-start.13) | collective-permute-done | bytes 24608 | tf_op jit(solution)/shard_map/ppermute | solution.py:148
  113.1 7.1 %collective-permute-done.14 = f32[3,2,1024]{2,1,0:T(2,128)S(1)} collective-permute-done((f32[3,2,1024]{2,1,0:T(2,128)S(1)}, f32[3,2,1024]{2,1,0:T(2,128)S(1)}, u32[]{:S(2)}, u32[]{:S(2)}) %collective-permute-start.14) | collective-permute-done | bytes 24608 | tf_op jit(solution)/shard_map/ppermute | solution.py:148
  121.0 1.3 collective-permute-start.18
  122.3 3.0 collective-permute-start.17
  129.7 1.3 collective-permute-start.20
  131.0 3.0 collective-permute-start.19
  139.1 1.3 collective-permute-start.22
  140.4 3.0 collective-permute-start.21
  145.3 1.3 collective-permute-start.24
  146.6 3.2 collective-permute-start.23
  154.1 1.3 collective-permute-start.26
  155.3 3.0 collective-permute-start.25
  162.8 1.3 fusion.41
  164.2 104.9 %all-reduce.3.cloned.1.call-done = f32[3,32,1024]{2,1,0:T(8,128)} async-done(((f32[3,32,1024]{2,1,0:T(8,128)}), f32[3,32,1024]{2,1,0:T(8,128)}) %all-reduce.3.cloned.1.call-update) | async-done | bytes 393232 | tf_op jit(solution)/shard_map/psum | solution.py:156
  269.1 1.1 fusion.500
  270.2 1.3 collective-permute-start.28
  271.5 3.0 collective-permute-start.27
  274.6 0.9 collective-permute-done.27
  279.0 1.3 collective-permute-start.30
  280.3 3.0 collective-permute-start.29
  283.3 0.9 collective-permute-done.29
  287.8 0.9 copy-done
  289.2 1.3 collective-permute-start.32
  290.5 3.2 collective-permute-start.31
  295.4 1.3 collective-permute-start.34
  296.7 3.0 collective-permute-start.33
  304.2 1.3 collective-permute-start.36
  305.5 3.0 collective-permute-start.35
  308.5 0.9 collective-permute-done.35
  312.9 1.3 fusion.23
  314.3 107.9 %all-reduce.5.cloned.1.call-done = f32[3,32,1024]{2,1,0:T(8,128)} async-done(((f32[3,32,1024]{2,1,0:T(8,128)}), f32[3,32,1024]{2,1,0:T(8,128)}) %all-reduce.5.cloned.1.call-update) | async-done | bytes 393232 | tf_op jit(solution)/shard_map/psum | solution.py:156
  422.1 1.5 multiply_add_fusion.1
  (383 shorter events, 35.7 us)
Async XLA Ops:
  7.2 91.5 %copy-start.1 = (f32[32,1024]{1,0:T(8,128)S(1)}, f32[32,1024]{1,0:T(8,128)}, u32[]{:S(2)}) copy-start(f32[32,1024]{1,0:T(8,128)} %param.6) | copy-start | bytes 393220
  7.2 261.9 %all-reduce.3.cloned.1.call-start = ((), (), s32[]{:S(2)}) async-start(), calls=%async_computation | async-start | bytes 786432 | tf_op jit(solution)/shard_map/psum | solution.py:156
  7.2 9.0 %collective-permute-start = (f32[3,2,1024]{2,1,0:T(2,128)}, f32[3,2,1024]{2,1,0:T(2,128)S(1)}, u32[]{:S(2)}, u32[]{:S(2)}) collective-permute-start(f32[3,2,1024]{2,1,0:T(2,128)} %param.5), channel_id=1, source_target_pairs={{0,2},{2,4},{4,6},{6,8},{8,10},{10,12},{12,14},{14,16},{16,18},{18... | collective-permute-start | bytes 73736 | tf_op jit(solution)/shard_map/ppermute | solution.py:148
  16.3 7.4 %collective-permute-start.1 = (f32[3,2,1024]{2,1,0:T(2,128)S(1)}, f32[3,2,1024]{2,1,0:T(2,128)S(1)}, u32[]{:S(2)}, u32[]{:S(2)}) collective-permute-start(f32[3,2,1024]{2,1,0:T(2,128)S(1)} %collective-permute-done), channel_id=1, source_target_pairs={{0,2},{2,4},{4,6},{6,8},{8,10},{10,12},{12,14},{14,16},{16,18},{18... | collective-permute-start | bytes 73736 | tf_op jit(solution)/shard_map/ppermute | solution.py:148
  23.7 7.4 %collective-permute-start.2 = (f32[3,2,1024]{2,1,0:T(2,128)S(1)}, f32[3,2,1024]{2,1,0:T(2,128)S(1)}, u32[]{:S(2)}, u32[]{:S(2)}) collective-permute-start(f32[3,2,1024]{2,1,0:T(2,128)S(1)} %collective-permute-done.1), channel_id=1, source_target_pairs={{0,2},{2,4},{4,6},{6,8},{8,10},{10,12},{12,14},{14,16},{16,18},{18... | collective-permute-start | bytes 73736 | tf_op jit(solution)/shard_map/ppermute | solution.py:148
  31.1 7.4 %collective-permute-start.3 = (f32[3,2,1024]{2,1,0:T(2,128)S(1)}, f32[3,2,1024]{2,1,0:T(2,128)S(1)}, u32[]{:S(2)}, u32[]{:S(2)}) collective-permute-start(f32[3,2,1024]{2,1,0:T(2,128)S(1)} %collective-permute-done.2), channel_id=1, source_target_pairs={{0,2},{2,4},{4,6},{6,8},{8,10},{10,12},{12,14},{14,16},{16,18},{18... | collective-permute-start | bytes 73736 | tf_op jit(solution)/shard_map/ppermute | solution.py:148
  38.5 7.4 %collective-permute-start.4 = (f32[3,2,1024]{2,1,0:T(2,128)S(1)}, f32[3,2,1024]{2,1,0:T(2,128)S(1)}, u32[]{:S(2)}, u32[]{:S(2)}) collective-permute-start(f32[3,2,1024]{2,1,0:T(2,128)S(1)} %collective-permute-done.3), channel_id=1, source_target_pairs={{0,2},{2,4},{4,6},{6,8},{8,10},{10,12},{12,14},{14,16},{16,18},{18... | collective-permute-start | bytes 73736 | tf_op jit(solution)/shard_map/ppermute | solution.py:148
  45.9 7.4 %collective-permute-start.5 = (f32[3,2,1024]{2,1,0:T(2,128)S(1)}, f32[3,2,1024]{2,1,0:T(2,128)S(1)}, u32[]{:S(2)}, u32[]{:S(2)}) collective-permute-start(f32[3,2,1024]{2,1,0:T(2,128)S(1)} %collective-permute-done.4), channel_id=1, source_target_pairs={{0,2},{2,4},{4,6},{6,8},{8,10},{10,12},{12,14},{14,16},{16,18},{18... | collective-permute-start | bytes 73736 | tf_op jit(solution)/shard_map/ppermute | solution.py:148
  53.4 7.4 %collective-permute-start.6 = (f32[3,2,1024]{2,1,0:T(2,128)S(1)}, f32[3,2,1024]{2,1,0:T(2,128)S(1)}, u32[]{:S(2)}, u32[]{:S(2)}) collective-permute-start(f32[3,2,1024]{2,1,0:T(2,128)S(1)} %collective-permute-done.5), channel_id=1, source_target_pairs={{0,2},{2,4},{4,6},{6,8},{8,10},{10,12},{12,14},{14,16},{16,18},{18... | collective-permute-start | bytes 73736 | tf_op jit(solution)/shard_map/ppermute | solution.py:148
  60.8 7.4 %collective-permute-start.7 = (f32[3,2,1024]{2,1,0:T(2,128)S(1)}, f32[3,2,1024]{2,1,0:T(2,128)S(1)}, u32[]{:S(2)}, u32[]{:S(2)}) collective-permute-start(f32[3,2,1024]{2,1,0:T(2,128)S(1)} %collective-permute-done.6), channel_id=1, source_target_pairs={{0,2},{2,4},{4,6},{6,8},{8,10},{10,12},{12,14},{14,16},{16,18},{18... | collective-permute-start | bytes 73736 | tf_op jit(solution)/shard_map/ppermute | solution.py:148
  68.2 7.4 %collective-permute-start.8 = (f32[3,2,1024]{2,1,0:T(2,128)S(1)}, f32[3,2,1024]{2,1,0:T(2,128)S(1)}, u32[]{:S(2)}, u32[]{:S(2)}) collective-permute-start(f32[3,2,1024]{2,1,0:T(2,128)S(1)} %collective-permute-done.7), channel_id=1, source_target_pairs={{0,2},{2,4},{4,6},{6,8},{8,10},{10,12},{12,14},{14,16},{16,18},{18... | collective-permute-start | bytes 73736 | tf_op jit(solution)/shard_map/ppermute | solution.py:148
  75.6 7.4 %collective-permute-start.9 = (f32[3,2,1024]{2,1,0:T(2,128)S(1)}, f32[3,2,1024]{2,1,0:T(2,128)S(1)}, u32[]{:S(2)}, u32[]{:S(2)}) collective-permute-start(f32[3,2,1024]{2,1,0:T(2,128)S(1)} %collective-permute-done.8), channel_id=1, source_target_pairs={{0,2},{2,4},{4,6},{6,8},{8,10},{10,12},{12,14},{14,16},{16,18},{18... | collective-permute-start | bytes 73736 | tf_op jit(solution)/shard_map/ppermute | solution.py:148
  83.1 7.5 %collective-permute-start.10 = (f32[3,2,1024]{2,1,0:T(2,128)S(1)}, f32[3,2,1024]{2,1,0:T(2,128)S(1)}, u32[]{:S(2)}, u32[]{:S(2)}) collective-permute-start(f32[3,2,1024]{2,1,0:T(2,128)S(1)} %collective-permute-done.9), channel_id=1, source_target_pairs={{0,2},{2,4},{4,6},{6,8},{8,10},{10,12},{12,14},{14,16},{16,18},{18... | collective-permute-start | bytes 73736 | tf_op jit(solution)/shard_map/ppermute | solution.py:148
  90.5 7.4 %collective-permute-start.11 = (f32[3,2,1024]{2,1,0:T(2,128)S(1)}, f32[3,2,1024]{2,1,0:T(2,128)S(1)}, u32[]{:S(2)}, u32[]{:S(2)}) collective-permute-start(f32[3,2,1024]{2,1,0:T(2,128)S(1)} %collective-permute-done.10), channel_id=1, source_target_pairs={{0,2},{2,4},{4,6},{6,8},{8,10},{10,12},{12,14},{14,16},{16,18},{18... | collective-permute-start | bytes 73736 | tf_op jit(solution)/shard_map/ppermute | solution.py:148
  98.0 7.4 %collective-permute-start.12 = (f32[3,2,1024]{2,1,0:T(2,128)S(1)}, f32[3,2,1024]{2,1,0:T(2,128)S(1)}, u32[]{:S(2)}, u32[]{:S(2)}) collective-permute-start(f32[3,2,1024]{2,1,0:T(2,128)S(1)} %collective-permute-done.11), channel_id=1, source_target_pairs={{0,2},{2,4},{4,6},{6,8},{8,10},{10,12},{12,14},{14,16},{16,18},{18... | collective-permute-start | bytes 73736 | tf_op jit(solution)/shard_map/ppermute | solution.py:148
  98.7 26.6 %collective-permute-start.16 = (f32[2,4,1024]{2,1,0:T(4,128)S(1)}, f32[2,4,1024]{2,1,0:T(4,128)S(1)}, u32[]{:S(2)}, u32[]{:S(2)}) collective-permute-start(f32[2,4,1024]{2,1,0:T(4,128)S(1)} %get-tuple-element.205), channel_id=1, source_target_pairs={{1,0},{3,2},{5,4},{7,6},{9,8},{11,10},{13,12},{15,14},{17,16},{19,... | collective-permute-start | bytes 98312 | tf_op jit(solution)/shard_map/ppermute | solution.py:22
  100.0 25.3 %collective-permute-start.15 = (f32[2,4,1024]{2,1,0:T(4,128)S(1)}, f32[2,4,1024]{2,1,0:T(4,128)S(1)}, u32[]{:S(2)}, u32[]{:S(2)}) collective-permute-start(f32[2,4,1024]{2,1,0:T(4,128)S(1)} %get-tuple-element.204), channel_id=1, source_target_pairs={{0,1},{2,3},{4,5},{6,7},{8,9},{10,11},{12,13},{14,15},{16,17},{18,... | collective-permute-start | bytes 98312 | tf_op jit(solution)/shard_map/ppermute | solution.py:21
  103.1 17.2 %copy-start.2 = (f32[3,2,1024]{2,1,0:T(2,128)S(1)}, f32[3,2,1024]{2,1,0:T(2,128)}, u32[]{:S(2)}) copy-start(f32[3,2,1024]{2,1,0:T(2,128)} %param.5) | copy-start | bytes 73732
  105.4 7.4 %collective-permute-start.13 = (f32[3,2,1024]{2,1,0:T(2,128)S(1)}, f32[3,2,1024]{2,1,0:T(2,128)S(1)}, u32[]{:S(2)}, u32[]{:S(2)}) collective-permute-start(f32[3,2,1024]{2,1,0:T(2,128)S(1)} %collective-permute-done.12), channel_id=1, source_target_pairs={{0,2},{2,4},{4,6},{6,8},{8,10},{10,12},{12,14},{14,16},{16,18},{18... | collective-permute-start | bytes 73736 | tf_op jit(solution)/shard_map/ppermute | solution.py:148
  112.8 7.4 %collective-permute-start.14 = (f32[3,2,1024]{2,1,0:T(2,128)S(1)}, f32[3,2,1024]{2,1,0:T(2,128)S(1)}, u32[]{:S(2)}, u32[]{:S(2)}) collective-permute-start(f32[3,2,1024]{2,1,0:T(2,128)S(1)} %collective-permute-done.13), channel_id=1, source_target_pairs={{0,2},{2,4},{4,6},{6,8},{8,10},{10,12},{12,14},{14,16},{16,18},{18... | collective-permute-start | bytes 73736 | tf_op jit(solution)/shard_map/ppermute | solution.py:148
  121.0 4.4 %collective-permute-start.18 = (f32[1,3,4,1024]{3,2,1,0:T(4,128)S(1)}, f32[1,3,4,1024]{3,2,1,0:T(4,128)S(1)}, u32[]{:S(2)}, u32[]{:S(2)}) collective-permute-start(f32[1,3,4,1024]{3,2,1,0:T(4,128)S(1)} %get-tuple-element.195), channel_id=1, source_target_pairs={{1,0},{3,2},{5,4},{7,6},{9,8},{11,10},{13,12},{15,14},{17,16},{19,... | collective-permute-start | bytes 147464 | tf_op jit(solution)/shard_map/ppermute | solution.py:22
  122.3 3.9 collective-permute-start.17
  129.7 5.3 %collective-permute-start.20 = (f32[2,3,4,1024]{3,2,1,0:T(4,128)S(1)}, f32[2,3,4,1024]{3,2,1,0:T(4,128)S(1)}, u32[]{:S(2)}, u32[]{:S(2)}) collective-permute-start(f32[2,3,4,1024]{3,2,1,0:T(4,128)S(1)} %get-tuple-element.91), channel_id=1, source_target_pairs={{1,0},{3,2},{5,4},{7,6},{9,8},{11,10},{13,12},{15,14},{17,16},{19,... | collective-permute-start | bytes 294920 | tf_op jit(solution)/shard_map/ppermute | solution.py:22
  131.0 4.0 collective-permute-start.19
  139.1 4.3 %collective-permute-start.22 = (f32[1,3,1,1024]{3,2,1,0:T(1,128)S(1)}, f32[1,3,1,1024]{3,2,1,0:T(1,128)S(1)}, u32[]{:S(2)}, u32[]{:S(2)}) collective-permute-start(f32[1,3,1,1024]{3,2,1,0:T(1,128)S(1)} %get-tuple-element.193), channel_id=1, source_target_pairs={{1,0},{3,2},{5,4},{7,6},{9,8},{11,10},{13,12},{15,14},{17,16},{19,... | collective-permute-start | bytes 36872 | tf_op jit(solution)/shard_map/ppermute | solution.py:22
  140.4 3.9 collective-permute-start.21
  145.3 4.5 %collective-permute-start.24 = (f32[1,3,4,1024]{3,2,1,0:T(4,128)S(1)}, f32[1,3,4,1024]{3,2,1,0:T(4,128)S(1)}, u32[]{:S(2)}, u32[]{:S(2)}) collective-permute-start(f32[1,3,4,1024]{3,2,1,0:T(4,128)S(1)} %get-tuple-element.191), channel_id=1, source_target_pairs={{1,0},{3,2},{5,4},{7,6},{9,8},{11,10},{13,12},{15,14},{17,16},{19,... | collective-permute-start | bytes 147464 | tf_op jit(solution)/shard_map/ppermute | solution.py:22
  146.6 3.9 collective-permute-start.23
  154.1 5.0 %collective-permute-start.26 = (f32[2,3,4,1024]{3,2,1,0:T(4,128)S(1)}, f32[2,3,4,1024]{3,2,1,0:T(4,128)S(1)}, u32[]{:S(2)}, u32[]{:S(2)}) collective-permute-start(f32[2,3,4,1024]{3,2,1,0:T(4,128)S(1)} %get-tuple-element.89), channel_id=1, source_target_pairs={{1,0},{3,2},{5,4},{7,6},{9,8},{11,10},{13,12},{15,14},{17,16},{19,... | collective-permute-start | bytes 294920 | tf_op jit(solution)/shard_map/ppermute | solution.py:22
  155.3 4.0 collective-permute-start.25
  164.1 258.0 %all-reduce.5.cloned.1.call-start = ((), (), s32[]{:S(2)}) async-start(), calls=%async_computation.1 | async-start | bytes 786432 | tf_op jit(solution)/shard_map/psum | solution.py:156
  270.2 4.3 %collective-permute-start.28 = (f32[1,3,4,1024]{3,2,1,0:T(4,128)S(1)}, f32[1,3,4,1024]{3,2,1,0:T(4,128)S(1)}, u32[]{:S(2)}, u32[]{:S(2)}) collective-permute-start(f32[1,3,4,1024]{3,2,1,0:T(4,128)S(1)} %get-tuple-element.189), channel_id=1, source_target_pairs={{1,0},{3,2},{5,4},{7,6},{9,8},{11,10},{13,12},{15,14},{17,16},{19,... | collective-permute-start | bytes 147464 | tf_op jit(solution)/shard_map/ppermute | solution.py:22
  271.5 3.9 collective-permute-start.27
  279.0 4.3 %collective-permute-start.30 = (f32[2,3,4,1024]{3,2,1,0:T(4,128)S(1)}, f32[2,3,4,1024]{3,2,1,0:T(4,128)S(1)}, u32[]{:S(2)}, u32[]{:S(2)}) collective-permute-start(f32[2,3,4,1024]{3,2,1,0:T(4,128)S(1)} %get-tuple-element.87), channel_id=1, source_target_pairs={{1,0},{3,2},{5,4},{7,6},{9,8},{11,10},{13,12},{15,14},{17,16},{19,... | collective-permute-start | bytes 294920 | tf_op jit(solution)/shard_map/ppermute | solution.py:22
  280.3 4.0 collective-permute-start.29
  287.6 1.0 copy-start
  289.2 4.6 %collective-permute-start.32 = (f32[1,3,1,1024]{3,2,1,0:T(1,128)S(1)}, f32[1,3,1,1024]{3,2,1,0:T(1,128)S(1)}, u32[]{:S(2)}, u32[]{:S(2)}) collective-permute-start(f32[1,3,1,1024]{3,2,1,0:T(1,128)S(1)} %get-tuple-element.187), channel_id=1, source_target_pairs={{1,0},{3,2},{5,4},{7,6},{9,8},{11,10},{13,12},{15,14},{17,16},{19,... | collective-permute-start | bytes 36872 | tf_op jit(solution)/shard_map/ppermute | solution.py:22
  290.5 3.9 collective-permute-start.31
  295.4 4.3 %collective-permute-start.34 = (f32[1,3,4,1024]{3,2,1,0:T(4,128)S(1)}, f32[1,3,4,1024]{3,2,1,0:T(4,128)S(1)}, u32[]{:S(2)}, u32[]{:S(2)}) collective-permute-start(f32[1,3,4,1024]{3,2,1,0:T(4,128)S(1)} %get-tuple-element.185), channel_id=1, source_target_pairs={{1,0},{3,2},{5,4},{7,6},{9,8},{11,10},{13,12},{15,14},{17,16},{19,... | collective-permute-start | bytes 147464 | tf_op jit(solution)/shard_map/ppermute | solution.py:22
  296.7 3.9 collective-permute-start.33
  304.2 4.3 %collective-permute-start.36 = (f32[2,3,4,1024]{3,2,1,0:T(4,128)S(1)}, f32[2,3,4,1024]{3,2,1,0:T(4,128)S(1)}, u32[]{:S(2)}, u32[]{:S(2)}) collective-permute-start(f32[2,3,4,1024]{3,2,1,0:T(4,128)S(1)} %get-tuple-element.85), channel_id=1, source_target_pairs={{1,0},{3,2},{5,4},{7,6},{9,8},{11,10},{13,12},{15,14},{17,16},{19,... | collective-permute-start | bytes 294920 | tf_op jit(solution)/shard_map/ppermute | solution.py:22
  305.5 4.0 collective-permute-start.35
Sparse Core Ops, SparseCore 0:
  164.2 104.7 all-reduce.2
  314.4 107.6 all-reduce.4
